TPU v7x, 128 devices: a whole 4x4x4 slice. The times are simulated.
128 devices in a mesh: dp: 16 (over z, x), seq: 8 (over y, core).
Axes of the slice: x: 4, y: 4, z: 4, core: 2. Of those that a mesh axis runs over, the one named last changes fastest.
Arguments:
- layer_input: bfloat16 [2, 16, 1024, 896], P(None, 'dp', 'seq'), may hold values from -6 to 6
- pic_start: int32 [2, 16], P(None, 'dp'), may hold values from 0 to 768, as said below
- norm_one: bfloat16 [896], P('dp'), may hold values from 0.099609375 to 1.8984375
- w_query: bfloat16 [896, 896], P('dp'), may hold values from -0.1875 to 0.1875
- b_query: bfloat16 [896], P('dp'), may hold values from -3 to 3
- w_key: bfloat16 [896, 128], P('dp'), may hold values from -0.1875 to 0.1875
- b_key: bfloat16 [128], P('dp'), may hold values from -3 to 3
- w_value: bfloat16 [896, 128], P('dp'), may hold values from -0.1875 to 0.1875
- b_value: bfloat16 [128], P('dp'), may hold values from -3 to 3
- w_out: bfloat16 [896, 896], P('dp'), may hold values from -1.5 to 1.5
- norm_two: bfloat16 [896], P('dp'), may hold values from 0.099609375 to 1.8984375
- w_gate: bfloat16 [896, 4864], P('dp'), may hold values from -0.1875 to 0.1875
- w_up: bfloat16 [896, 4864], P('dp'), may hold values from -0.1875 to 0.1875
- w_down: bfloat16 [4864, 896], P('dp'), may hold values from -0.078125 to 0.078125
- out_grad: bfloat16 [2, 16, 1024, 896], P(None, 'dp', 'seq'), may hold values from -6 to 6
Outputs:
- layer_output: bfloat16 [2, 16, 1024, 896], P(None, 'dp', 'seq')
- input_grad: float32 [2, 16, 1024, 896], P(None, 'dp', 'seq')
- norm_one_grad: float32 [896], P('dp')
- w_query_grad: float32 [896, 896], P('dp')
- b_query_grad: float32 [896], P('dp')
- w_key_grad: float32 [896, 128], P('dp')
- b_key_grad: float32 [128], P('dp')
- w_value_grad: float32 [896, 128], P('dp')
- b_value_grad: float32 [128], P('dp')
- w_out_grad: float32 [896, 896], P('dp')
- norm_two_grad: float32 [896], P('dp')
- w_gate_grad: float32 [896, 4864], P('dp')
- w_up_grad: float32 [896, 4864], P('dp')
- w_down_grad: float32 [4864, 896], P('dp')
Inputs may be any that keep to these rules, and one draw needn't show every extreme that they name: Each sequence has one picture block of 256 tokens starting at its pic_start, a multiple of 256.
All inputs are finite; a program needn't handle non-finite values.
Results may differ from a plain program's by a relative error of at most 0.028.
Values may be sent and summed in bfloat16 or wider, within the bound.
A program may use at most 192 MiB of HBM per device.

v0:
```python
import jax
import jax.numpy as jnp
from jax import lax
from jax.sharding import PartitionSpec as P

HEADS = 14
KV_HEADS = 2
HD = 64
PIC = 256
EPSILON = 1e-06
ROPE_BASE = 1000000.0
NEGATIVE = -1e30


def rope_tables(positions, head_dim):
    half_dim = head_dim // 2
    exponent = jnp.arange(half_dim, dtype=jnp.float32) * (2.0 / head_dim)
    inverse = ROPE_BASE ** (-exponent)
    angles = positions.astype(jnp.float32)[:, None] * inverse[None, :]
    angles = jnp.concatenate([angles, angles], axis=1)
    return (jnp.cos(angles), jnp.sin(angles))


def rotate_half(inputs, head_dim):
    shaped = inputs.reshape(inputs.shape[:-1] + (inputs.shape[-1] // head_dim, 2, head_dim // 2))
    turned = jnp.stack([-shaped[..., 1, :], shaped[..., 0, :]], axis=-2)
    return turned.reshape(inputs.shape)


def rotate(inputs, cosine, sine, head_dim, direction):
    count = inputs.shape[-1] // head_dim
    cos_all = jnp.tile(cosine, (1, count))
    sin_all = jnp.tile(sine, (1, count))
    return inputs * cos_all + direction * rotate_half(inputs, head_dim) * sin_all


def visible_mask(query_pos, key_pos, start):
    inside_query = (query_pos >= start) & (query_pos < start + PIC)
    inside_key = (key_pos >= start) & (key_pos < start + PIC)
    return (key_pos[None, :] <= query_pos[:, None]) | inside_query[:, None] & inside_key[None, :]


def norm_rows(inputs, gain_row):
    inverse = lax.rsqrt(jnp.mean(inputs * inputs, axis=-1, keepdims=True) + EPSILON)
    return (inverse, inputs * inverse * gain_row)


def norm_back(inputs, inverse, gain_row, grad_normed):
    scaled_in = inputs * inverse
    gain_grad = jnp.sum(grad_normed * scaled_in, axis=0)
    weighted = grad_normed * gain_row
    grad_in = inverse * weighted - scaled_in * inverse * jnp.mean(
        weighted * scaled_in, axis=-1, keepdims=True
    )
    return (grad_in, gain_grad)


def outer_sum(left, right):
    return jnp.einsum("ta,tb->ab", left, right, preferred_element_type=jnp.float32)


def back_dot(grad_rows, weight):
    return jnp.einsum("tb,ab->ta", grad_rows, weight, preferred_element_type=jnp.float32)


def per_device(
    layer_input,
    pic_start,
    norm_one,
    w_query,
    b_query,
    w_key,
    b_key,
    w_value,
    b_value,
    w_out,
    norm_two,
    w_gate,
    w_up,
    w_down,
    out_grad,
):
    micro_count, seq_count, row_count, model_width = layer_input.shape
    length = row_count * lax.axis_size("seq")
    tokens = seq_count * row_count
    group = HEADS // KV_HEADS
    score_scale = HD ** (-0.5)
    query_pos = lax.axis_index("seq") * row_count + jnp.arange(row_count, dtype=jnp.int32)
    key_pos = jnp.arange(length, dtype=jnp.int32)
    cosine, sine = rope_tables(jnp.tile(query_pos, seq_count), HD)

    def scores_of(query_heads, key_heads, start):
        scores = (
            jnp.einsum("rkgd,lkd->kgrl", query_heads, key_heads, preferred_element_type=jnp.float32)
            * score_scale
        )
        return jnp.where(visible_mask(query_pos, key_pos, start), scores, NEGATIVE)

    def attend_forward(element):
        q_seq, k_seq, v_seq, start = element
        query_heads = q_seq.reshape(row_count, KV_HEADS, group, HD)
        key_heads = k_seq.reshape(length, KV_HEADS, HD)
        value_heads = v_seq.reshape(length, KV_HEADS, HD)
        masked = scores_of(query_heads, key_heads, start)
        row_max = jnp.max(masked, axis=-1, keepdims=True)
        unnormed = jnp.exp(masked - row_max)
        row_total = jnp.sum(unnormed, axis=-1, keepdims=True)
        probs = (unnormed / row_total).astype(jnp.bfloat16)
        attended = jnp.einsum(
            "kgrl,lkd->rkgd", probs, value_heads, preferred_element_type=jnp.float32
        )
        return (
            attended.reshape(row_count, HEADS * HD).astype(jnp.bfloat16),
            row_max + jnp.log(row_total),
        )

    def attend_backward(element):
        q_seq, k_seq, v_seq, start, log_total, grad_seq = element
        query_heads = q_seq.reshape(row_count, KV_HEADS, group, HD)
        key_heads = k_seq.reshape(length, KV_HEADS, HD)
        value_heads = v_seq.reshape(length, KV_HEADS, HD)
        grad_heads = grad_seq.reshape(row_count, KV_HEADS, group, HD)
        probs = jnp.exp(scores_of(query_heads, key_heads, start) - log_total)
        rounded = probs.astype(jnp.bfloat16)
        prob_grad = jnp.einsum(
            "rkgd,lkd->kgrl", grad_heads, value_heads, preferred_element_type=jnp.float32
        )
        centre = jnp.sum(probs * prob_grad, axis=-1, keepdims=True)
        score_grad = (probs * (prob_grad - centre)).astype(jnp.bfloat16)
        query_grad = (
            jnp.einsum("kgrl,lkd->rkgd", score_grad, key_heads, preferred_element_type=jnp.float32)
            * score_scale
        )
        key_grad = (
            jnp.einsum(
                "kgrl,rkgd->lkd", score_grad, query_heads, preferred_element_type=jnp.float32
            )
            * score_scale
        )
        value_grad = jnp.einsum(
            "kgrl,rkgd->lkd", rounded, grad_heads, preferred_element_type=jnp.float32
        )
        return (
            query_grad.reshape(row_count, HEADS * HD),
            key_grad.reshape(length, KV_HEADS * HD),
            value_grad.reshape(length, KV_HEADS * HD),
        )

    totals = None
    outputs = []
    input_grads = []
    for micro_index in range(micro_count):
        attn_full = (
            lax.all_gather(norm_one, "dp", axis=0, tiled=True),
            lax.all_gather(w_query, "dp", axis=0, tiled=True),
            lax.all_gather(b_query, "dp", axis=0, tiled=True),
            lax.all_gather(w_key, "dp", axis=0, tiled=True),
            lax.all_gather(b_key, "dp", axis=0, tiled=True),
            lax.all_gather(w_value, "dp", axis=0, tiled=True),
            lax.all_gather(b_value, "dp", axis=0, tiled=True),
            lax.all_gather(w_out, "dp", axis=0, tiled=True),
        )
        mlp_full = (
            lax.all_gather(norm_two, "dp", axis=0, tiled=True),
            lax.all_gather(w_gate, "dp", axis=0, tiled=True),
            lax.all_gather(w_up, "dp", axis=0, tiled=True),
            lax.all_gather(w_down, "dp", axis=0, tiled=True),
        )
        gain_one, query_full, qbias_full, key_full, kbias_full, value_full, vbias_full, out_full = (
            attn_full
        )
        inputs = layer_input[micro_index].reshape(tokens, model_width).astype(jnp.float32)
        inv_one, normed_float = norm_rows(inputs, gain_one.astype(jnp.float32))
        normed = normed_float.astype(jnp.bfloat16)
        query_lin = jnp.dot(
            normed, query_full, preferred_element_type=jnp.float32
        ) + qbias_full.astype(jnp.float32)
        key_lin = jnp.dot(normed, key_full, preferred_element_type=jnp.float32) + kbias_full.astype(
            jnp.float32
        )
        value_lin = jnp.dot(
            normed, value_full, preferred_element_type=jnp.float32
        ) + vbias_full.astype(jnp.float32)
        queries = rotate(query_lin, cosine, sine, HD, 1.0).astype(jnp.bfloat16)
        keys = rotate(key_lin, cosine, sine, HD, 1.0).astype(jnp.bfloat16)
        values = value_lin.astype(jnp.bfloat16)
        keys_all, values_all = (
            lax.all_gather(
                keys.reshape(seq_count, row_count, KV_HEADS * HD), "seq", axis=1, tiled=True
            ),
            lax.all_gather(
                values.reshape(seq_count, row_count, KV_HEADS * HD), "seq", axis=1, tiled=True
            ),
        )
        query_seqs = queries.reshape(seq_count, row_count, HEADS * HD)
        starts = pic_start[micro_index]
        attended, log_total = lax.map(attend_forward, (query_seqs, keys_all, values_all, starts))
        att_rows = attended.reshape(tokens, HEADS * HD)
        resid = inputs + jnp.dot(att_rows, out_full, preferred_element_type=jnp.float32)
        gain_two, gate_full, up_full, down_full = mlp_full
        inv_two, normed_two_float = norm_rows(resid, gain_two.astype(jnp.float32))
        normed_two = normed_two_float.astype(jnp.bfloat16)
        gate_float = lax.optimization_barrier(
            jnp.dot(normed_two, gate_full, preferred_element_type=jnp.float32).astype(jnp.bfloat16)
        ).astype(jnp.float32)
        up_float = lax.optimization_barrier(
            jnp.dot(normed_two, up_full, preferred_element_type=jnp.float32).astype(jnp.bfloat16)
        ).astype(jnp.float32)
        sigmoid_gate = jax.nn.sigmoid(gate_float)
        hidden = (gate_float * sigmoid_gate * up_float).astype(jnp.bfloat16)
        output = resid + jnp.dot(hidden, down_full, preferred_element_type=jnp.float32)
        outputs.append(output.astype(jnp.bfloat16).reshape(seq_count, row_count, model_width))
        attn_back = (
            lax.all_gather(norm_one, "dp", axis=0, tiled=True),
            lax.all_gather(w_query, "dp", axis=0, tiled=True),
            lax.all_gather(b_query, "dp", axis=0, tiled=True),
            lax.all_gather(w_key, "dp", axis=0, tiled=True),
            lax.all_gather(b_key, "dp", axis=0, tiled=True),
            lax.all_gather(w_value, "dp", axis=0, tiled=True),
            lax.all_gather(b_value, "dp", axis=0, tiled=True),
            lax.all_gather(w_out, "dp", axis=0, tiled=True),
        )
        mlp_back = (
            lax.all_gather(norm_two, "dp", axis=0, tiled=True),
            lax.all_gather(w_gate, "dp", axis=0, tiled=True),
            lax.all_gather(w_up, "dp", axis=0, tiled=True),
            lax.all_gather(w_down, "dp", axis=0, tiled=True),
        )
        (
            gain_one_back,
            query_back,
            qbias_back,
            key_back,
            kbias_back,
            value_back,
            vbias_back,
            out_back,
        ) = attn_back
        gain_two_back, gate_back, up_back, down_back = mlp_back
        grad_rows = out_grad[micro_index].reshape(tokens, model_width)
        down_grad = outer_sum(hidden, grad_rows)
        hidden_grad = lax.optimization_barrier(
            back_dot(grad_rows, down_back).astype(jnp.bfloat16)
        ).astype(jnp.float32)
        gate_grad_low = (
            hidden_grad * up_float * sigmoid_gate * (1.0 + gate_float * (1.0 - sigmoid_gate))
        ).astype(jnp.bfloat16)
        up_grad_low = (hidden_grad * gate_float * sigmoid_gate).astype(jnp.bfloat16)
        gate_wgrad = outer_sum(normed_two, gate_grad_low)
        up_wgrad = outer_sum(normed_two, up_grad_low)
        grad_normed_two = back_dot(gate_grad_low, gate_back) + back_dot(up_grad_low, up_back)
        grad_middle, gain_two_grad = norm_back(
            resid, inv_two, gain_two_back.astype(jnp.float32), grad_normed_two
        )
        resid_grad = grad_rows.astype(jnp.float32) + grad_middle
        attn_grad_low = resid_grad.astype(jnp.bfloat16)
        out_wgrad = outer_sum(att_rows, attn_grad_low)
        heads_grad = back_dot(attn_grad_low, out_back).astype(jnp.bfloat16)
        query_grad, key_part, value_part = lax.map(
            attend_backward,
            (
                query_seqs,
                keys_all,
                values_all,
                starts,
                log_total,
                heads_grad.reshape(seq_count, row_count, HEADS * HD),
            ),
        )
        key_grad, value_grad = (
            lax.psum_scatter(
                key_part.astype(jnp.bfloat16), "seq", scatter_dimension=1, tiled=True
            ).astype(jnp.float32),
            lax.psum_scatter(
                value_part.astype(jnp.bfloat16), "seq", scatter_dimension=1, tiled=True
            ).astype(jnp.float32),
        )
        qlin_grad = rotate(query_grad.reshape(tokens, HEADS * HD), cosine, sine, HD, -1.0).astype(
            jnp.bfloat16
        )
        klin_grad = rotate(key_grad.reshape(tokens, KV_HEADS * HD), cosine, sine, HD, -1.0).astype(
            jnp.bfloat16
        )
        vlin_grad = value_grad.reshape(tokens, KV_HEADS * HD).astype(jnp.bfloat16)
        grad_normed = (
            back_dot(qlin_grad, query_back)
            + back_dot(klin_grad, key_back)
            + back_dot(vlin_grad, value_back)
        )
        grad_first, gain_one_grad = norm_back(
            inputs, inv_one, gain_one_back.astype(jnp.float32), grad_normed
        )
        input_grads.append((resid_grad + grad_first).reshape(seq_count, row_count, model_width))
        batch_grads = (
            gain_one_grad,
            outer_sum(normed, qlin_grad),
            jnp.sum(qlin_grad.astype(jnp.float32), axis=0),
            outer_sum(normed, klin_grad),
            jnp.sum(klin_grad.astype(jnp.float32), axis=0),
            outer_sum(normed, vlin_grad),
            jnp.sum(vlin_grad.astype(jnp.float32), axis=0),
            out_wgrad,
            gain_two_grad,
            gate_wgrad,
            up_wgrad,
            down_grad,
        )
        totals = batch_grads if totals is None else jax.tree.map(jnp.add, totals, batch_grads)
    shares = (
        lax.psum_scatter(totals[0], "dp", scatter_dimension=0, tiled=True),
        lax.psum_scatter(totals[1], "dp", scatter_dimension=0, tiled=True),
        lax.psum_scatter(totals[2], "dp", scatter_dimension=0, tiled=True),
        lax.psum_scatter(totals[3], "dp", scatter_dimension=0, tiled=True),
        lax.psum_scatter(totals[4], "dp", scatter_dimension=0, tiled=True),
        lax.psum_scatter(totals[5], "dp", scatter_dimension=0, tiled=True),
        lax.psum_scatter(totals[6], "dp", scatter_dimension=0, tiled=True),
        lax.psum_scatter(totals[7], "dp", scatter_dimension=0, tiled=True),
        lax.psum_scatter(totals[8], "dp", scatter_dimension=0, tiled=True),
        lax.psum_scatter(totals[9], "dp", scatter_dimension=0, tiled=True),
        lax.psum_scatter(totals[10], "dp", scatter_dimension=0, tiled=True),
        lax.psum_scatter(totals[11], "dp", scatter_dimension=0, tiled=True),
    )
    shares = (
        lax.psum(shares[0].astype(jnp.bfloat16), "seq").astype(jnp.float32),
        lax.psum(shares[1].astype(jnp.bfloat16), "seq").astype(jnp.float32),
        lax.psum(shares[2].astype(jnp.bfloat16), "seq").astype(jnp.float32),
        lax.psum(shares[3].astype(jnp.bfloat16), "seq").astype(jnp.float32),
        lax.psum(shares[4].astype(jnp.bfloat16), "seq").astype(jnp.float32),
        lax.psum(shares[5].astype(jnp.bfloat16), "seq").astype(jnp.float32),
        lax.psum(shares[6].astype(jnp.bfloat16), "seq").astype(jnp.float32),
        lax.psum(shares[7].astype(jnp.bfloat16), "seq").astype(jnp.float32),
        lax.psum(shares[8].astype(jnp.bfloat16), "seq").astype(jnp.float32),
        lax.psum(shares[9].astype(jnp.bfloat16), "seq").astype(jnp.float32),
        lax.psum(shares[10].astype(jnp.bfloat16), "seq").astype(jnp.float32),
        lax.psum(shares[11].astype(jnp.bfloat16), "seq").astype(jnp.float32),
    )
    return (
        jnp.stack(outputs),
        jnp.stack(input_grads),
        shares[0],
        shares[1],
        shares[2],
        shares[3],
        shares[4],
        shares[5],
        shares[6],
        shares[7],
        shares[8],
        shares[9],
        shares[10],
        shares[11],
    )


def solution(mesh):
    placed = (
        P(None, "dp", "seq", None),
        P(None, "dp"),
        P("dp"),
        P("dp", None),
        P("dp"),
        P("dp", None),
        P("dp"),
        P("dp", None),
        P("dp"),
        P("dp", None),
        P("dp"),
        P("dp", None),
        P("dp", None),
        P("dp", None),
        P(None, "dp", "seq", None),
    )
    return jax.shard_map(
        per_device,
        mesh=mesh,
        in_specs=placed,
        out_specs=(
            P(None, "dp", "seq", None),
            P(None, "dp", "seq", None),
            P("dp"),
            P("dp", None),
            P("dp"),
            P("dp", None),
            P("dp"),
            P("dp", None),
            P("dp"),
            P("dp", None),
            P("dp"),
            P("dp", None),
            P("dp", None),
            P("dp", None),
        ),
        check_vma=False,
    )
```

profile of v0, /device:TPU:0, one launch (start us, length us, event | category | flops | bytes accessed | tf_op | source)
XLA Modules:
  0.0 1245.0 jit_solution(1288814986106040895)
XLA Ops:
  20.1 42.5 %all-reduce.18 = (bf16[128]{0:T(256)(128)(2,1)S(1)}, bf16[896]{0:T(1024)(128)(2,1)S(1)}, bf16[128]{0:T(256)(128)(2,1)S(1)}, bf16[896]{0:T(1024)(128)(2,1)S(1)}, bf16[896]{0:T(1024)(128)(2,1)S(1)}) all-reduce(bf16[128]{0:T(256)(128)(2,1)S(1)} %dynamic-update-slice.1, ...), channel_id=1, replica_groups=mesh['dp'=16,'seq'=8] {'dp'}, use_global_device_ids=true, to_apply=%add.1 | all-reduce | flops 2944 | bytes 11776
  62.6 21.6 %all_gather.33 = bf16[896,128]{1,0:T(8,128)(2,1)S(1)} all-gather(bf16[56,128]{1,0:T(8,128)(2,1)} %param.22), channel_id=1, replica_groups=mesh['dp'=16,'seq'=8] {'dp'}, dimensions={0}, use_global_device_ids=true | all-gather | bytes 243712 | tf_op jit(solution)/shard_map/all_gather | solution.py:159
  84.7 13.2 %all-gather = bf16[1024,128]{1,0:T(8,128)(2,1)S(1)} all-gather(bf16[128,128]{1,0:T(8,128)(2,1)S(1)} %fusion.60), channel_id=2, replica_groups=mesh['dp'=16,'seq'=8] {'seq'}, dimensions={0}, use_global_device_ids=true | all-gather | bytes 294912 | tf_op jit(solution)/shard_map/all_gather | solution.py:191
  99.0 12.8 %all-gather.2 = bf16[1024,128]{1,0:T(8,128)(2,1)S(1)} all-gather(bf16[128,128]{1,0:T(8,128)(2,1)S(1)} %fusion.61), channel_id=4, replica_groups=mesh['dp'=16,'seq'=8] {'seq'}, dimensions={0}, use_global_device_ids=true | all-gather | bytes 294912 | tf_op jit(solution)/shard_map/all_gather | solution.py:191
  115.0 23.1 %all_gather.36 = bf16[896,128]{1,0:T(8,128)(2,1)S(1)} all-gather(bf16[56,128]{1,0:T(8,128)(2,1)S(1)} %copy-done.68), channel_id=1, replica_groups=mesh['dp'=16,'seq'=8] {'dp'}, dimensions={0}, use_global_device_ids=true | all-gather | bytes 243712 | tf_op jit(solution)/shard_map/all_gather | solution.py:157
  141.4 11.5 all-gather.1
  152.9 13.2 %all-gather.3 = bf16[1024,128]{0,1:T(8,128)(2,1)} all-gather(bf16[128,128]{0,1:T(8,128)(2,1)S(1)} %get-tuple-element.209), channel_id=5, replica_groups=mesh['dp'=16,'seq'=8] {'seq'}, dimensions={0}, use_global_device_ids=true | all-gather | bytes 294912 | tf_op jit(solution)/shard_map/all_gather | solution.py:188
  184.8 2.7 multiply_reduce_fusion.4
  194.2 7.4 convolution_convert_fusion
  201.6 2.5 convolution_convert_fusion.1
  204.1 46.5 %all-gather.16.cloned.1.call-done = bf16[896,4864]{1,0:T(8,128)(2,1)} async-done(((bf16[56,4864]{1,0:T(8,128)(2,1)}), bf16[896,4864]{1,0:T(8,128)(2,1)}) %all-gather.16.cloned.1.call-update) | async-done | bytes 8716304 | tf_op jit(solution)/shard_map/all_gather | solution.py:166
  250.6 4.9 convolution_convert_fusion.4
  255.5 69.0 %all-gather.14.cloned.1.call-done = bf16[896,4864]{1,0:T(8,128)(2,1)} async-done(((bf16[56,4864]{1,0:T(8,128)(2,1)}), bf16[896,4864]{1,0:T(8,128)(2,1)}) %all-gather.14.cloned.1.call-update) | async-done | bytes 8716304 | tf_op jit(solution)/shard_map/all_gather | solution.py:165
  324.6 5.1 convolution_convert_fusion.5
  329.7 7.4 fusion.168
  337.2 4.7 multiply_reduce_fusion.1
  345.2 3.0 fusion.164
  348.2 3.0 multiply_reduce_fusion
  353.7 2.1 convolution_convert_fusion.7
  356.7 7.5 fusion
  364.2 4.6 fusion.2
  370.6 2.9 fusion.53
  376.0 7.7 fusion.3
  383.7 4.6 fusion.5
  390.2 2.9 fusion.52
  395.2 4.6 fusion.49
  401.0 4.4 fusion.46
  408.2 3.2 convolution_add_fusion.3
  412.4 2.9 broadcast_multiply_fusion.2
  418.9 2.4 convolution_add_fusion.4
  422.6 10.4 fusion.166
  433.0 14.6 %convolution_add_fusion.2 = f32[896,4864]{1,0:T(8,128)} fusion(f32[896,4864]{1,0:T(8,128)} %fusion.166, bf16[128,896]{1,0:T(8,128)(2,1)S(1)} %copy-done.26, bf16[128,4864]{1,0:T(8,128)(2,1)S(1)} %copy-done.18, bf16[128,4864]{1,0:T(8,128)(2,1)S(1)} %copy-done.24, bf16[128,4864]{1,0:T(8,128)(2,1)S(1)} %convolution_convert_fusion.3), kind=kOutput, calls=%fused_computation.2 | convolution fusion | flops 1128136704 | bytes 38830080 | tf_op jit(solution)/shard_map/ta,tb->ab/dot_general | solution.py:59
  447.6 4.1 fusion.156
  451.8 10.3 convolution_add_fusion.1
  462.4 4.3 fusion.104
  466.6 10.4 convolution_add_fusion
  480.5 5.3 fusion.59
  493.0 8.2 reduce-scatter.40.cloned.1.call-done
  507.0 74.5 %reduce-scatter.48.cloned.1.call-done = f32[56,896]{1,0:T(8,128)} async-done(((f32[896,896]{1,0:T(8,128)}), f32[56,896]{1,0:T(8,128)}) %reduce-scatter.48.cloned.1.call-update) | async-done | bytes 200720
  583.1 79.3 %reduce-scatter.42.cloned.1.call-done = f32[56,896]{1,0:T(8,128)} async-done(((f32[896,896]{1,0:T(8,128)}), f32[56,896]{1,0:T(8,128)}) %reduce-scatter.42.cloned.1.call-update) | async-done | bytes 200720
  663.9 115.4 %reduce-scatter.50.cloned.1.call-done = f32[56,4864]{1,0:T(8,128)} async-done(((f32[896,4864]{1,0:T(8,128)}), f32[56,4864]{1,0:T(8,128)}) %reduce-scatter.50.cloned.1.call-update) | async-done | bytes 1089552
  781.4 115.7 %reduce-scatter.52.cloned.1.call-done = f32[56,4864]{1,0:T(8,128)} async-done(((f32[896,4864]{1,0:T(8,128)}), f32[56,4864]{1,0:T(8,128)}) %reduce-scatter.52.cloned.1.call-update) | async-done | bytes 1089552
  899.2 115.2 %reduce-scatter.54.cloned.1.call-done = f32[304,896]{1,0:T(8,128)} async-done(((f32[4864,896]{1,0:T(8,128)}), f32[304,896]{1,0:T(8,128)}) %reduce-scatter.54.cloned.1.call-update) | async-done | bytes 1089552
  1016.6 72.3 %all-reduce.17 = (bf16[896]{0:T(1024)(128)(2,1)S(1)}, bf16[896]{0:T(1024)(128)(2,1)S(1)}, bf16[128]{0:T(256)(128)(2,1)S(1)}, bf16[128]{0:T(256)(128)(2,1)S(1)}, bf16[896]{0:T(1024)(128)(2,1)S(1)}) all-reduce(f32[896]{0:T(1024)S(1)} %add.367, f32[896]{0:T(1024)S(1)} %add.372, ...), channel_id=10, replica_groups=mesh['dp'=16,'seq'=8] {'dp'}, use_global_device_ids=true, to_apply=%region_20.21.clone | all-reduce | flops 2944 | bytes 17664
  1091.3 71.1 %reduce-scatter.44.cloned.1.call-done = f32[56,128]{1,0:T(8,128)} async-done(((f32[896,128]{1,0:T(8,128)}), f32[56,128]{1,0:T(8,128)}) %reduce-scatter.44.cloned.1.call-update) | async-done | bytes 28688
  1163.1 23.7 %all-reduce.19 = (bf16[56]{0:T(256)(128)(2,1)S(1)}, bf16[56]{0:T(256)(128)(2,1)S(1)}, bf16[56,128]{1,0:T(8,128)(2,1)S(1)}, bf16[8]{0:T(256)(128)(2,1)S(1)}, bf16...) all-reduce(bf16[56]{0:T(256)(128)(2,1)S(1)} %dynamic-slice.44, ...), channel_id=1, replica_groups=mesh['dp'=16,'seq'=8] {'seq'}, use_global_device_ids=true, to_apply=%region_21.22 | all-reduce | flops 14520 | bytes 58080 | tf_op jit(solution)/shard_map/psum | solution.py:324
  1190.6 40.1 %all-reduce.23.cloned.1.call-done = (bf16[56,896]{1,0:T(8,128)(2,1)}, bf16[56,896]{1,0:T(8,128)(2,1)}, bf16[56,4864]{1,0:T(8,128)(2,1)}, bf16[56,4864]{1,0:T(8,128)(2,1)}, bf16[304,896]{1,0:T(8,128)(2,1)}) async-done(((bf16[56,896]{1,0:T(8,128)(2,1)}, bf16[56,896]{1,0:T(8,128)(2,1)}, bf16[56,4864]{1,0:T(8,128)(2,1)}, bf16[56,4864]{1,0:T(8,128)(2,1)}, bf16[304,896]{1,0:T(8,128)(2,1)}), ...) | async-done | bytes 1835024 | tf_op jit(solution)/shard_map/psum | solution.py:325
  1234.0 2.1 convert_element_type.548
  (368 shorter events, 104.3 us)
Async XLA Ops:
  7.2 77.0 %copy-start.12 = (bf16[2,1,128,896]{3,2,1,0:T(8,128)(2,1)S(1)}, bf16[2,1,128,896]{3,2,1,0:T(8,128)(2,1)}, u32[]{:S(2)}) copy-start(bf16[2,1,128,896]{3,2,1,0:T(8,128)(2,1)} %param.15) | copy-start | bytes 1376260
  7.2 160.0 %all-gather.10.cloned.1.call-start = ((), (), s32[]{:S(2)}) async-start(), calls=%async_computation.11 | async-start | bytes 1705984 | tf_op jit(solution)/shard_map/all_gather | solution.py:155
  7.9 176.9 %all-gather.12.cloned.1.call-start = ((), (), s32[]{:S(2)}) async-start(), calls=%async_computation.12 | async-start | bytes 1705984 | tf_op jit(solution)/shard_map/all_gather | solution.py:161
  8.7 185.2 %all-gather.18.cloned.1.call-start = ((), (), s32[]{:S(2)}) async-start(), calls=%async_computation.15 | async-start | bytes 9261056 | tf_op jit(solution)/shard_map/all_gather | solution.py:167
  9.4 241.2 %all-gather.16.cloned.1.call-start = ((), (), s32[]{:S(2)}) async-start(), calls=%async_computation.14 | async-start | bytes 9261056 | tf_op jit(solution)/shard_map/all_gather | solution.py:166
  10.0 314.6 %all-gather.14.cloned.1.call-start = ((), (), s32[]{:S(2)}) async-start(), calls=%async_computation.13 | async-start | bytes 9261056 | tf_op jit(solution)/shard_map/all_gather | solution.py:165
  10.6 479.5 %reduce-scatter.38.cloned.1.call-start = ((), (), s32[]{:S(2)}) async-start(), calls=%async_computation.18 | async-start | bytes 294912
  84.2 28.5 %copy-start.63 = (bf16[896,128]{1,0:T(8,128)(2,1)}, bf16[896,128]{1,0:T(8,128)(2,1)S(1)}, u32[]{:S(2)}) copy-start(bf16[896,128]{1,0:T(8,128)(2,1)S(1)} %all_gather.33) | copy-start | bytes 688132
  97.9 17.1 %copy-start.68 = (bf16[56,128]{1,0:T(8,128)(2,1)S(1)}, bf16[56,128]{1,0:T(8,128)(2,1)}, u32[]{:S(2)}) copy-start(bf16[56,128]{1,0:T(8,128)(2,1)} %param.20) | copy-start | bytes 43012
  112.9 25.9 %copy-start.54 = (f32[128,64]{0,1:T(8,128)}, f32[128,64]{0,1:T(8,128)S(1)}, u32[]{:S(2)}) copy-start(f32[128,64]{0,1:T(8,128)S(1)} %get-tuple-element.216) | copy-start | bytes 98308
  112.9 25.9 %copy-start.56 = (f32[128,64]{0,1:T(8,128)}, f32[128,64]{0,1:T(8,128)S(1)}, u32[]{:S(2)}) copy-start(f32[128,64]{0,1:T(8,128)S(1)} %get-tuple-element.217) | copy-start | bytes 98308
  152.9 34.6 %copy-start.40 = (bf16[1024,128]{0,1:T(8,128)(2,1)}, bf16[1024,128]{0,1:T(8,128)(2,1)S(1)}, u32[]{:S(2)}) copy-start(bf16[1024,128]{0,1:T(8,128)(2,1)S(1)} %all-gather.1) | copy-start | bytes 786436
  179.0 8.6 copy-start.48
  193.1 8.6 copy-start.65
  193.7 8.0 copy-start.38
  194.2 7.4 copy-start.2
  204.1 133.1 %copy-start.22 = (bf16[128,4864]{1,0:T(8,128)(2,1)}, bf16[128,4864]{1,0:T(8,128)(2,1)S(1)}, u32[]{:S(2)}) copy-start(bf16[128,4864]{1,0:T(8,128)(2,1)S(1)} %convolution_convert_fusion.1) | copy-start | bytes 3735556
  255.5 74.1 %copy-start.20 = (bf16[128,4864]{1,0:T(8,128)(2,1)}, bf16[128,4864]{1,0:T(8,128)(2,1)S(1)}, u32[]{:S(2)}) copy-start(bf16[128,4864]{1,0:T(8,128)(2,1)S(1)} %convolution_convert_fusion.4) | copy-start | bytes 3735556
  324.5 12.6 %slice-start.4 = ((s8[8716288]{0:T(1024)(128)(4,1)}), s8[4194304]{0:T(1024)(128)(4,1)S(1)}, s32[]{:S(2)}) async-start(s8[8716288]{0:T(1024)(128)(4,1)} %bitcast.431), calls=%async_computation.32 | async-start | bytes 8388608
  324.5 12.6 %slice-start.5 = ((s8[8716288]{0:T(1024)(128)(4,1)}), s8[4194304]{0:T(1024)(128)(4,1)S(1)}, s32[]{:S(2)}) async-start(s8[8716288]{0:T(1024)(128)(4,1)} %bitcast.431), calls=%async_computation.33 | async-start | bytes 8388608
  329.7 7.5 copy-start.14
  329.7 7.5 slice-start.6
  329.7 7.5 copy-start.39
  329.7 7.5 copy-start.52
  345.2 87.7 %copy-start.6 = (bf16[128,4864]{1,0:T(8,128)(2,1)}, bf16[128,4864]{1,0:T(8,128)(2,1)S(1)}, u32[]{:S(2)}) copy-start(bf16[128,4864]{1,0:T(8,128)(2,1)S(1)} %convolution_convert_fusion.3) | copy-start | bytes 3735556
  353.7 10.4 copy-start.44
  356.7 7.5 slice-start
  356.7 7.5 slice-start.1
  375.5 115.5 %reduce-scatter.34.cloned.1.call-start = ((), (), s32[]{:S(2)}) async-start(), calls=%async_computation.16 | async-start | bytes 294912
  376.0 7.7 slice-start.2
  376.0 7.7 slice-start.3
  395.1 96.9 %reduce-scatter.36.cloned.1.call-start = ((), (), s32[]{:S(2)}) async-start(), calls=%async_computation.17 | async-start | bytes 294912
  400.9 100.2 %reduce-scatter.40.cloned.1.call-start = ((), (), s32[]{:S(2)}) async-start(), calls=%async_computation.19 | async-start | bytes 294912
  406.6 174.9 %reduce-scatter.48.cloned.1.call-start = ((), (), s32[]{:S(2)}) async-start(), calls=%async_computation.23 | async-start | bytes 3411968
  411.4 250.9 %reduce-scatter.42.cloned.1.call-start = ((), (), s32[]{:S(2)}) async-start(), calls=%async_computation.20 | async-start | bytes 3411968
  421.3 11.7 copy-start.26
  421.3 358.0 %reduce-scatter.50.cloned.1.call-start = ((), (), s32[]{:S(2)}) async-start(), calls=%async_computation.24 | async-start | bytes 18522112
  422.6 10.4 copy-start.18
  422.6 10.4 copy-start.24
  447.6 449.5 %reduce-scatter.52.cloned.1.call-start = ((), (), s32[]{:S(2)}) async-start(), calls=%async_computation.25 | async-start | bytes 18522112
  462.1 552.2 %reduce-scatter.54.cloned.1.call-start = ((), (), s32[]{:S(2)}) async-start(), calls=%async_computation.26 | async-start | bytes 18522112
  477.1 8.8 slice-start.10
  477.1 613.5 %reduce-scatter.46.cloned.1.call-start = ((), (), s32[]{:S(2)}) async-start(), calls=%async_computation.22 | async-start | bytes 487424
  488.9 13.3 %copy-start.13 = (bf16[2,1,128,896]{3,2,1,0:T(8,128)(2,1)S(1)}, bf16[2,1,128,896]{3,2,1,0:T(8,128)(2,1)}, u32[]{:S(2)}) copy-start(bf16[2,1,128,896]{3,2,1,0:T(8,128)(2,1)} %param.15) | copy-start | bytes 1376260
  503.6 658.8 %reduce-scatter.44.cloned.1.call-start = ((), (), s32[]{:S(2)}) async-start(), calls=%async_computation.21 | async-start | bytes 487424
  505.3 725.4 %all-reduce.23.cloned.1.call-start = ((), (), s32[]{:S(2)}) async-start(), calls=%async_computation.27 | async-start | bytes 3670016 | tf_op jit(solution)/shard_map/psum | solution.py:325
  781.4 307.9 %copy-start.29 = (f32[128,896]{1,0:T(8,128)S(1)}, f32[128,896]{1,0:T(8,128)}, u32[]{:S(2)}) copy-start(f32[128,896]{1,0:T(8,128)} %copy-done.27) | copy-start | bytes 1376260
  781.4 307.9 %copy-start.32 = (f32[128,896]{1,0:T(8,128)S(1)}, f32[128,896]{1,0:T(8,128)}, u32[]{:S(2)}) copy-start(f32[128,896]{1,0:T(8,128)} %copy-done.30) | copy-start | bytes 1376260
  (52 other events, 173.6 us)
Sparse Core Ops, SparseCore 0:
  10.2 46.6 all-gather.9
  59.0 43.4 all-gather.11
  104.7 71.8 all-gather.17
  178.6 71.9 all-gather.15
  252.6 71.9 all-gather.13
  375.7 30.0 reduce-scatter.37
  408.3 29.3 reduce-scatter.33
  440.0 29.3 reduce-scatter.35
  471.8 29.3 reduce-scatter.39
  504.5 76.9 reduce-scatter.47
  585.0 77.3 reduce-scatter.41
  665.7 113.5 reduce-scatter.49
  783.1 113.8 reduce-scatter.51
  900.4 113.9 reduce-scatter.53
  1017.7 70.8 reduce-scatter.45
  1091.7 70.6 reduce-scatter.43
  1166.3 64.3 all-reduce.22
where the time goes:
time: 1250 us; the launch traced here: 1240 us
  waiting for transfers between devices  738 us (59%)
  blocking collectives  234 us (19%)
  matrix products  164 us (13%)
  other arithmetic  48 us (4%)
  local copies, waits for them, and re-layouts  39.6 us (3%)
  between operations  19.9 us (2%)
    unnamed x28, waiting for transfers between devices  583 us
    unnamed x2, blocking collectives  115 us
    all_gather x1, waiting for transfers between devices, per_device(): lax.all_gather(w_gate, 'dp', axis=0, tiled=True)  69 us
    dot_general x14, matrix products, outer_sum(): jnp.einsum('ta,tb->ab', left, right, preferred_element_type=jnp.float32)  64.8 us
    all_gather x1, waiting for transfers between devices, per_device(): lax.all_gather(w_up, 'dp', axis=0, tiled=True)  46.5 us
    psum x1, waiting for transfers between devices, per_device(): lax.psum(shares[1].astype(jnp.bfloat16), 'seq').astype(jnp.float32)  40.1 us
    dot_general x14, matrix products, back_dot(): jnp.einsum('tb,ab->ta', grad_rows, weight, preferred_element_type=jnp.flo...  33.1 us
    unnamed x198, local copies, waits for them, and re-layouts  28 us
  transfers between devices with their start and end apart: 17, of which 10 were waited for; matrix products, arithmetic and copies ran while one was open for 15% of the time, Pallas kernels for 0%

commit v1 on v0

--- a/solution.py
+++ b/solution.py
@@ -1,3 +1,4 @@
+import functools
 import jax
 import jax.numpy as jnp
 from jax import lax
@@ -10,6 +11,36 @@
 EPSILON = 1e-06
 ROPE_BASE = 1000000.0
 NEGATIVE = -1e30
+
+
+def column_remake(sample, d0):
+    far_arr = lax.axis_index("seq")
+    d_next = lax.axis_size("seq")
+    oldest, local_part, earlier = (d_next, far_arr, sample.shape[d0])
+    buffer = tuple(((i0, (i0 + 1) % oldest) for i0 in range(oldest)))
+    steps_seen = tuple(((i0, (i0 - 1) % oldest) for i0 in range(oldest)))
+    q_next = jnp.zeros(
+        (*sample.shape[:d0], oldest * earlier, *sample.shape[d0 + 1 :]), sample.dtype
+    )
+    w1 = response = sample
+    newest = oldest // 2
+    k = 1
+    q_next = lax.dynamic_update_slice_in_dim(q_next, sample, local_part * earlier, axis=d0)
+    while k < newest + 1:
+        w1 = lax.ppermute(w1, axis_name="seq", perm=buffer)
+        q_next = lax.dynamic_update_slice_in_dim(
+            q_next, w1, (local_part - k) % oldest * earlier, axis=d0
+        )
+        if k < oldest - newest:
+            response = lax.ppermute(response, axis_name="seq", perm=steps_seen)
+            q_next = lax.dynamic_update_slice_in_dim(
+                q_next, response, (local_part + k) % oldest * earlier, axis=d0
+            )
+        k += 1
+    return q_next
+
+
+counts_try_all = functools.partial(column_remake, d0=1)
 
 
 def rope_tables(positions, head_dim):
@@ -188,9 +219,7 @@
             lax.all_gather(
                 keys.reshape(seq_count, row_count, KV_HEADS * HD), "seq", axis=1, tiled=True
             ),
-            lax.all_gather(
-                values.reshape(seq_count, row_count, KV_HEADS * HD), "seq", axis=1, tiled=True
-            ),
+            counts_try_all(values.reshape(seq_count, row_count, KV_HEADS * HD)),
         )
         query_seqs = queries.reshape(seq_count, row_count, HEADS * HD)
         starts = pic_start[micro_index]

time: 1250 us -> 1250 us (level)
  blocking collectives: 234 us -> 208 us
  starting transfers between devices: 1.73 us -> 14.8 us
  waiting for transfers between devices: 738 us -> 751 us
    all_gather x2 -> x0, blocking collectives: 26 us -> none  [per_device(): lax.all_gather(values.reshape(seq_count, row_count, KV_HEADS * HD), 'seq'...]
    ppermute x0 -> x14, starting transfers between devices: none -> 13.1 us  [the longest x6 12.6 us: column_remake(): response = lax.ppermute(response, axis_name='seq', perm=steps_seen)]
    unnamed x198 -> x204, local copies, waits for them, and re-layouts: 28 us -> 28.5 us
  transfers between devices with their start and end apart: 17 -> 31, of which waited for: 10 -> 14; matrix products, arithmetic and copies ran while one was open for 15% -> 15% of each run, Pallas kernels for 0% -> 0%
where the time goes in v1:
time: 1250 us; the launch traced here: 1240 us
  waiting for transfers between devices  751 us (60%)
  blocking collectives  208 us (17%)
  matrix products  164 us (13%)
  other arithmetic  49.2 us (4%)
  local copies, waits for them, and re-layouts  37.9 us (3%)
  between operations  20.1 us (2%)
  starting transfers between devices  14.8 us (1%)
    unnamed x28, waiting for transfers between devices  583 us
    unnamed x2, blocking collectives  115 us
    all_gather x1, waiting for transfers between devices, per_device(): lax.all_gather(w_gate, 'dp', axis=0, tiled=True)  69 us
    dot_general x14, matrix products, outer_sum(): jnp.einsum('ta,tb->ab', left, right, preferred_element_type=jnp.float32)  64.8 us
    all_gather x1, waiting for transfers between devices, per_device(): lax.all_gather(w_up, 'dp', axis=0, tiled=True)  50.5 us
    psum x1, waiting for transfers between devices, per_device(): lax.psum(shares[1].astype(jnp.bfloat16), 'seq').astype(jnp.float32)  40 us
    dot_general x14, matrix products, back_dot(): jnp.einsum('tb,ab->ta', grad_rows, weight, preferred_element_type=jnp.flo...  32.7 us
    unnamed x204, local copies, waits for them, and re-layouts  28.5 us
  transfers between devices with their start and end apart: 31, of which 14 were waited for; matrix products, arithmetic and copies ran while one was open for 15% of the time, Pallas kernels for 0%

profile of v1, /device:TPU:0, one launch (start us, length us, event | category | flops | bytes accessed | tf_op | source)
XLA Modules:
  0.0 1244.7 jit_solution(11971223825559390602)
XLA Ops:
  17.5 42.5 %all-reduce.18 = (bf16[128]{0:T(256)(128)(2,1)S(1)}, bf16[896]{0:T(1024)(128)(2,1)S(1)}, bf16[128]{0:T(256)(128)(2,1)S(1)}, bf16[896]{0:T(1024)(128)(2,1)S(1)}, bf16[896]{0:T(1024)(128)(2,1)S(1)}) all-reduce(bf16[128]{0:T(256)(128)(2,1)S(1)} %dynamic-update-slice.1, ...), channel_id=1, replica_groups=mesh['dp'=16,'seq'=8] {'dp'}, use_global_device_ids=true, to_apply=%add.1 | all-reduce | flops 2944 | bytes 11776
  60.0 21.4 %all_gather.29 = bf16[896,128]{1,0:T(8,128)(2,1)S(1)} all-gather(bf16[56,128]{1,0:T(8,128)(2,1)} %param.22), channel_id=1, replica_groups=mesh['dp'=16,'seq'=8] {'dp'}, dimensions={0}, use_global_device_ids=true | all-gather | bytes 243712 | tf_op jit(solution)/shard_map/all_gather | solution.py:190
  84.0 2.7 collective-permute-start.1
  88.7 23.3 %all_gather.31 = bf16[896,128]{1,0:T(8,128)(2,1)S(1)} all-gather(bf16[56,128]{1,0:T(8,128)(2,1)S(1)} %copy-done.70), channel_id=1, replica_groups=mesh['dp'=16,'seq'=8] {'dp'}, dimensions={0}, use_global_device_ids=true | all-gather | bytes 243712 | tf_op jit(solution)/shard_map/all_gather | solution.py:188
  115.6 11.5 all-gather
  128.1 13.2 %all-gather.1 = bf16[1024,128]{0,1:T(8,128)(2,1)} all-gather(bf16[128,128]{0,1:T(8,128)(2,1)S(1)} %get-tuple-element.209), channel_id=3, replica_groups=mesh['dp'=16,'seq'=8] {'seq'}, dimensions={0}, use_global_device_ids=true | all-gather | bytes 294912 | tf_op jit(solution)/shard_map/all_gather | solution.py:219
  144.3 3.0 collective-permute-start.3
  147.4 3.0 collective-permute-start.12
  150.4 3.0 collective-permute-start.5
  154.9 3.0 collective-permute-done.4
  159.5 2.9 collective-permute-done.6
  180.9 2.7 multiply_reduce_fusion.4
  190.3 7.3 convolution_convert_fusion
  200.1 50.5 %all-gather.14.cloned.1.call-done = bf16[896,4864]{1,0:T(8,128)(2,1)} async-done(((bf16[56,4864]{1,0:T(8,128)(2,1)}), bf16[896,4864]{1,0:T(8,128)(2,1)}) %all-gather.14.cloned.1.call-update) | async-done | bytes 8716304 | tf_op jit(solution)/shard_map/all_gather | solution.py:197
  250.5 4.9 convolution_convert_fusion.4
  255.5 69.0 %all-gather.12.cloned.1.call-done = bf16[896,4864]{1,0:T(8,128)(2,1)} async-done(((bf16[56,4864]{1,0:T(8,128)(2,1)}), bf16[896,4864]{1,0:T(8,128)(2,1)}) %all-gather.12.cloned.1.call-update) | async-done | bytes 8716304 | tf_op jit(solution)/shard_map/all_gather | solution.py:196
  324.5 5.1 convolution_convert_fusion.5
  329.7 7.4 fusion.168
  337.2 4.7 multiply_reduce_fusion.1
  345.2 2.7 fusion.164
  348.0 3.0 multiply_reduce_fusion
  356.4 7.5 fusion
  363.9 4.6 fusion.2
  370.3 2.9 fusion.53
  375.7 7.7 fusion.3
  383.5 4.6 fusion.5
  389.9 2.9 fusion.52
  394.9 4.6 fusion.49
  400.8 4.4 fusion.46
  407.9 3.2 convolution_add_fusion.3
  412.1 2.9 broadcast_multiply_fusion.2
  422.3 10.3 fusion.166
  432.7 14.6 %convolution_add_fusion.2 = f32[896,4864]{1,0:T(8,128)} fusion(f32[896,4864]{1,0:T(8,128)} %fusion.166, bf16[128,896]{1,0:T(8,128)(2,1)S(1)} %copy-done.26, bf16[128,4864]{1,0:T(8,128)(2,1)S(1)} %copy-done.18, bf16[128,4864]{1,0:T(8,128)(2,1)S(1)} %copy-done.24, bf16[128,4864]{1,0:T(8,128)(2,1)S(1)} %convolution_convert_fusion.3), kind=kOutput, calls=%fused_computation.2 | convolution fusion | flops 1128136704 | bytes 38830080 | tf_op jit(solution)/shard_map/ta,tb->ab/dot_general | solution.py:90
  447.3 4.1 fusion.156
  451.5 10.3 convolution_add_fusion.1
  462.1 4.3 fusion.104
  466.4 10.4 convolution_add_fusion
  480.2 5.3 fusion.59
  492.7 8.2 reduce-scatter.40.cloned.1.call-done
  506.7 74.4 %reduce-scatter.48.cloned.1.call-done = f32[56,896]{1,0:T(8,128)} async-done(((f32[896,896]{1,0:T(8,128)}), f32[56,896]{1,0:T(8,128)}) %reduce-scatter.48.cloned.1.call-update) | async-done | bytes 200720
  582.8 79.3 %reduce-scatter.42.cloned.1.call-done = f32[56,896]{1,0:T(8,128)} async-done(((f32[896,896]{1,0:T(8,128)}), f32[56,896]{1,0:T(8,128)}) %reduce-scatter.42.cloned.1.call-update) | async-done | bytes 200720
  663.7 115.4 %reduce-scatter.50.cloned.1.call-done = f32[56,4864]{1,0:T(8,128)} async-done(((f32[896,4864]{1,0:T(8,128)}), f32[56,4864]{1,0:T(8,128)}) %reduce-scatter.50.cloned.1.call-update) | async-done | bytes 1089552
  781.2 115.7 %reduce-scatter.52.cloned.1.call-done = f32[56,4864]{1,0:T(8,128)} async-done(((f32[896,4864]{1,0:T(8,128)}), f32[56,4864]{1,0:T(8,128)}) %reduce-scatter.52.cloned.1.call-update) | async-done | bytes 1089552
  898.9 115.2 %reduce-scatter.54.cloned.1.call-done = f32[304,896]{1,0:T(8,128)} async-done(((f32[4864,896]{1,0:T(8,128)}), f32[304,896]{1,0:T(8,128)}) %reduce-scatter.54.cloned.1.call-update) | async-done | bytes 1089552
  1016.4 72.3 %all-reduce.17 = (bf16[896]{0:T(1024)(128)(2,1)S(1)}, bf16[896]{0:T(1024)(128)(2,1)S(1)}, bf16[128]{0:T(256)(128)(2,1)S(1)}, bf16[128]{0:T(256)(128)(2,1)S(1)}, bf16[896]{0:T(1024)(128)(2,1)S(1)}) all-reduce(f32[896]{0:T(1024)S(1)} %add.462, f32[896]{0:T(1024)S(1)} %add.467, ...), channel_id=8, replica_groups=mesh['dp'=16,'seq'=8] {'dp'}, use_global_device_ids=true, to_apply=%region_20.21.clone | all-reduce | flops 2944 | bytes 17664
  1091.1 71.1 %reduce-scatter.44.cloned.1.call-done = f32[56,128]{1,0:T(8,128)} async-done(((f32[896,128]{1,0:T(8,128)}), f32[56,128]{1,0:T(8,128)}) %reduce-scatter.44.cloned.1.call-update) | async-done | bytes 28688
  1162.9 23.7 %all-reduce.19 = (bf16[56]{0:T(256)(128)(2,1)S(1)}, bf16[56]{0:T(256)(128)(2,1)S(1)}, bf16[56,128]{1,0:T(8,128)(2,1)S(1)}, bf16[8]{0:T(256)(128)(2,1)S(1)}, bf16...) all-reduce(bf16[56]{0:T(256)(128)(2,1)S(1)} %dynamic-slice.44, ...), channel_id=1, replica_groups=mesh['dp'=16,'seq'=8] {'seq'}, use_global_device_ids=true, to_apply=%region_21.22 | all-reduce | flops 14520 | bytes 58080 | tf_op jit(solution)/shard_map/psum | solution.py:353
  1190.4 40.0 %all-reduce.23.cloned.1.call-done = (bf16[56,896]{1,0:T(8,128)(2,1)}, bf16[56,896]{1,0:T(8,128)(2,1)}, bf16[56,4864]{1,0:T(8,128)(2,1)}, bf16[56,4864]{1,0:T(8,128)(2,1)}, bf16[304,896]{1,0:T(8,128)(2,1)}) async-done(((bf16[56,896]{1,0:T(8,128)(2,1)}, bf16[56,896]{1,0:T(8,128)(2,1)}, bf16[56,4864]{1,0:T(8,128)(2,1)}, bf16[56,4864]{1,0:T(8,128)(2,1)}, bf16[304,896]{1,0:T(8,128)(2,1)}), ...) | async-done | bytes 1835024 | tf_op jit(solution)/shard_map/psum | solution.py:354
  (414 shorter events, 117.7 us)
Async XLA Ops:
  7.2 75.6 %copy-start.12 = (bf16[2,1,128,896]{3,2,1,0:T(8,128)(2,1)S(1)}, bf16[2,1,128,896]{3,2,1,0:T(8,128)(2,1)}, u32[]{:S(2)}) copy-start(bf16[2,1,128,896]{3,2,1,0:T(8,128)(2,1)} %param.15) | copy-start | bytes 1376260
  7.2 79.6 %copy-start.72 = (s32[2,1]{0,1:T(1,128)S(1)}, s32[2,1]{0,1:T(1,128)}, u32[]{:S(2)}) copy-start(s32[2,1]{0,1:T(1,128)} %param.16) | copy-start | bytes 28
  7.2 81.4 %copy-start.70 = (bf16[56,128]{1,0:T(8,128)(2,1)S(1)}, bf16[56,128]{1,0:T(8,128)(2,1)}, u32[]{:S(2)}) copy-start(bf16[56,128]{1,0:T(8,128)(2,1)} %param.20) | copy-start | bytes 43012
  7.2 156.0 %all-gather.8.cloned.1.call-start = ((), (), s32[]{:S(2)}) async-start(), calls=%async_computation.11 | async-start | bytes 1705984 | tf_op jit(solution)/shard_map/all_gather | solution.py:186
  7.9 172.9 %all-gather.10.cloned.1.call-start = ((), (), s32[]{:S(2)}) async-start(), calls=%async_computation.12 | async-start | bytes 1705984 | tf_op jit(solution)/shard_map/all_gather | solution.py:192
  8.7 181.3 %all-gather.16.cloned.1.call-start = ((), (), s32[]{:S(2)}) async-start(), calls=%async_computation.15 | async-start | bytes 9261056 | tf_op jit(solution)/shard_map/all_gather | solution.py:198
  9.4 241.1 %all-gather.14.cloned.1.call-start = ((), (), s32[]{:S(2)}) async-start(), calls=%async_computation.14 | async-start | bytes 9261056 | tf_op jit(solution)/shard_map/all_gather | solution.py:197
  10.0 314.5 %all-gather.12.cloned.1.call-start = ((), (), s32[]{:S(2)}) async-start(), calls=%async_computation.13 | async-start | bytes 9261056 | tf_op jit(solution)/shard_map/all_gather | solution.py:196
  10.6 479.2 %reduce-scatter.38.cloned.1.call-start = ((), (), s32[]{:S(2)}) async-start(), calls=%async_computation.18 | async-start | bytes 294912
  81.4 31.5 %copy-start.65 = (bf16[896,128]{1,0:T(8,128)(2,1)}, bf16[896,128]{1,0:T(8,128)(2,1)S(1)}, u32[]{:S(2)}) copy-start(bf16[896,128]{1,0:T(8,128)(2,1)S(1)} %all_gather.29) | copy-start | bytes 688132
  83.1 60.2 %collective-permute-start.8 = (bf16[1,128,128]{1,2,0:T(8,128)(2,1)S(1)}, bf16[1,128,128]{1,2,0:T(8,128)(2,1)S(1)}, u32[]{:S(2)}, u32[]{:S(2)}) collective-permute-start(bf16[1,128,128]{1,2,0:T(8,128)(2,1)S(1)} %bitcast.523), channel_id=1, source_target_pairs={{0,7},{1,0},{2,1},{3,2},{4,3},{5,4},{6,5},{7,6},{8,15},{9,8},{10,9... | collective-permute-start | bytes 98312 | tf_op jit(solution)/shard_map/ppermute | solution.py:35
  83.1 61.2 %collective-permute-start.7 = (bf16[1,128,128]{1,2,0:T(8,128)(2,1)S(1)}, bf16[1,128,128]{1,2,0:T(8,128)(2,1)S(1)}, u32[]{:S(2)}, u32[]{:S(2)}) collective-permute-start(bf16[1,128,128]{1,2,0:T(8,128)(2,1)S(1)} %bitcast.524), channel_id=1, source_target_pairs={{0,1},{1,2},{2,3},{3,4},{4,5},{5,6},{6,7},{7,0},{8,9},{9,10},{10,1... | collective-permute-start | bytes 98312 | tf_op jit(solution)/shard_map/ppermute | solution.py:30
  84.0 60.3 %collective-permute-start.1 = (bf16[1,128,128]{1,2,0:T(8,128)(2,1)S(1)}, bf16[1,128,128]{1,2,0:T(8,128)(2,1)S(1)}, u32[]{:S(2)}, u32[]{:S(2)}) collective-permute-start(bf16[1,128,128]{1,2,0:T(8,128)(2,1)S(1)} %bitcast.525), channel_id=1, source_target_pairs={{0,7},{1,0},{2,1},{3,2},{4,3},{5,4},{6,5},{7,6},{8,15},{9,8},{10,9... | collective-permute-start | bytes 98312 | tf_op jit(solution)/shard_map/ppermute | solution.py:35
  86.7 60.5 %collective-permute-start = (bf16[1,128,128]{1,2,0:T(8,128)(2,1)S(1)}, bf16[1,128,128]{1,2,0:T(8,128)(2,1)S(1)}, u32[]{:S(2)}, u32[]{:S(2)}) collective-permute-start(bf16[1,128,128]{1,2,0:T(8,128)(2,1)S(1)} %bitcast.526), channel_id=1, source_target_pairs={{0,1},{1,2},{2,3},{3,4},{4,5},{5,6},{6,7},{7,0},{8,9},{9,10},{10,1... | collective-permute-start | bytes 98312 | tf_op jit(solution)/shard_map/ppermute | solution.py:30
  112.9 45.1 %copy-start.54 = (f32[128,64]{0,1:T(8,128)}, f32[128,64]{0,1:T(8,128)S(1)}, u32[]{:S(2)}) copy-start(f32[128,64]{0,1:T(8,128)S(1)} %get-tuple-element.216) | copy-start | bytes 98308
  112.9 45.1 %copy-start.56 = (f32[128,64]{0,1:T(8,128)}, f32[128,64]{0,1:T(8,128)S(1)}, u32[]{:S(2)}) copy-start(f32[128,64]{0,1:T(8,128)S(1)} %get-tuple-element.217) | copy-start | bytes 98308
  127.1 56.5 %copy-start.40 = (bf16[1024,128]{0,1:T(8,128)(2,1)}, bf16[1024,128]{0,1:T(8,128)(2,1)S(1)}, u32[]{:S(2)}) copy-start(bf16[1024,128]{0,1:T(8,128)(2,1)S(1)} %all-gather) | copy-start | bytes 786436
  143.3 4.0 collective-permute-start.10
  144.3 6.0 collective-permute-start.9
  144.3 6.0 collective-permute-start.3
  147.3 6.0 collective-permute-start.2
  147.4 10.5 collective-permute-start.12
  150.4 4.6 collective-permute-start.11
  150.4 7.6 collective-permute-start.5
  153.3 4.6 collective-permute-start.4
  154.9 4.6 collective-permute-start.13
  157.9 4.6 collective-permute-start.6
  200.0 137.1 %copy-start.22 = (bf16[128,4864]{1,0:T(8,128)(2,1)}, bf16[128,4864]{1,0:T(8,128)(2,1)S(1)}, u32[]{:S(2)}) copy-start(bf16[128,4864]{1,0:T(8,128)(2,1)S(1)} %convolution_convert_fusion.1) | copy-start | bytes 3735556
  255.5 74.1 %copy-start.20 = (bf16[128,4864]{1,0:T(8,128)(2,1)}, bf16[128,4864]{1,0:T(8,128)(2,1)S(1)}, u32[]{:S(2)}) copy-start(bf16[128,4864]{1,0:T(8,128)(2,1)S(1)} %convolution_convert_fusion.4) | copy-start | bytes 3735556
  324.5 12.6 %slice-start.4 = ((s8[8716288]{0:T(1024)(128)(4,1)}), s8[4194304]{0:T(1024)(128)(4,1)S(1)}, s32[]{:S(2)}) async-start(s8[8716288]{0:T(1024)(128)(4,1)} %bitcast.465), calls=%async_computation.32 | async-start | bytes 8388608
  324.5 12.6 %slice-start.5 = ((s8[8716288]{0:T(1024)(128)(4,1)}), s8[4194304]{0:T(1024)(128)(4,1)S(1)}, s32[]{:S(2)}) async-start(s8[8716288]{0:T(1024)(128)(4,1)} %bitcast.465), calls=%async_computation.33 | async-start | bytes 8388608
  345.2 87.5 %copy-start.6 = (bf16[128,4864]{1,0:T(8,128)(2,1)}, bf16[128,4864]{1,0:T(8,128)(2,1)S(1)}, u32[]{:S(2)}) copy-start(bf16[128,4864]{1,0:T(8,128)(2,1)S(1)} %convolution_convert_fusion.3) | copy-start | bytes 3735556
  353.4 10.5 copy-start.44
  375.3 115.5 %reduce-scatter.34.cloned.1.call-start = ((), (), s32[]{:S(2)}) async-start(), calls=%async_computation.16 | async-start | bytes 294912
  394.9 96.9 %reduce-scatter.36.cloned.1.call-start = ((), (), s32[]{:S(2)}) async-start(), calls=%async_computation.17 | async-start | bytes 294912
  400.7 100.2 %reduce-scatter.40.cloned.1.call-start = ((), (), s32[]{:S(2)}) async-start(), calls=%async_computation.19 | async-start | bytes 294912
  406.3 174.9 %reduce-scatter.48.cloned.1.call-start = ((), (), s32[]{:S(2)}) async-start(), calls=%async_computation.23 | async-start | bytes 3411968
  411.2 250.9 %reduce-scatter.42.cloned.1.call-start = ((), (), s32[]{:S(2)}) async-start(), calls=%async_computation.20 | async-start | bytes 3411968
  421.1 11.6 copy-start.26
  421.1 358.0 %reduce-scatter.50.cloned.1.call-start = ((), (), s32[]{:S(2)}) async-start(), calls=%async_computation.24 | async-start | bytes 18522112
  447.3 449.5 %reduce-scatter.52.cloned.1.call-start = ((), (), s32[]{:S(2)}) async-start(), calls=%async_computation.25 | async-start | bytes 18522112
  461.8 552.3 %reduce-scatter.54.cloned.1.call-start = ((), (), s32[]{:S(2)}) async-start(), calls=%async_computation.26 | async-start | bytes 18522112
  476.8 613.5 %reduce-scatter.46.cloned.1.call-start = ((), (), s32[]{:S(2)}) async-start(), calls=%async_computation.22 | async-start | bytes 487424
  488.6 13.3 %copy-start.13 = (bf16[2,1,128,896]{3,2,1,0:T(8,128)(2,1)S(1)}, bf16[2,1,128,896]{3,2,1,0:T(8,128)(2,1)}, u32[]{:S(2)}) copy-start(bf16[2,1,128,896]{3,2,1,0:T(8,128)(2,1)} %param.15) | copy-start | bytes 1376260
  503.4 658.8 %reduce-scatter.44.cloned.1.call-start = ((), (), s32[]{:S(2)}) async-start(), calls=%async_computation.21 | async-start | bytes 487424
  505.1 725.3 %all-reduce.23.cloned.1.call-start = ((), (), s32[]{:S(2)}) async-start(), calls=%async_computation.27 | async-start | bytes 3670016 | tf_op jit(solution)/shard_map/psum | solution.py:354
  781.2 307.9 %copy-start.29 = (f32[128,896]{1,0:T(8,128)S(1)}, f32[128,896]{1,0:T(8,128)}, u32[]{:S(2)}) copy-start(f32[128,896]{1,0:T(8,128)} %copy-done.27) | copy-start | bytes 1376260
  781.2 307.9 %copy-start.32 = (f32[128,896]{1,0:T(8,128)S(1)}, f32[128,896]{1,0:T(8,128)}, u32[]{:S(2)}) copy-start(f32[128,896]{1,0:T(8,128)} %copy-done.30) | copy-start | bytes 1376260
  (69 other events, 300.0 us)
Sparse Core Ops, SparseCore 0:
  10.2 46.5 all-gather.7
  58.9 43.5 all-gather.9
  104.7 71.8 all-gather.15
  178.5 71.9 all-gather.13
  252.5 71.9 all-gather.11
  375.4 30.0 reduce-scatter.37
  408.0 29.3 reduce-scatter.33
  439.7 29.2 reduce-scatter.35
  471.5 29.3 reduce-scatter.39
  504.2 76.9 reduce-scatter.47
  584.6 77.3 reduce-scatter.41
  665.4 113.6 reduce-scatter.49
  782.9 113.8 reduce-scatter.51
  900.1 113.9 reduce-scatter.53
  1017.5 70.9 reduce-scatter.45
  1091.5 70.5 reduce-scatter.43
  1166.1 64.2 all-reduce.22
